TPU v7x, 32 devices: a whole 2x2x4 slice. The times are simulated.
32 devices in a mesh: vis: 4 (over y, core), row: 4 (over z), col: 2 (over x).
Axes of the slice: x: 2, y: 2, z: 4, core: 2. Of those that a mesh axis runs over, the one named last changes fastest.
Arguments:
- images: bfloat16 [128, 6400], P(('vis', 'row', 'col')), may hold values from -6 to 6
- counts: int32 [4], replicated, may hold values from 1 to 32, 64 in all
- block_order: int32 [4], replicated, may hold values from 0 to 3, each once
- projector_norm_gain: float32 [6400], replicated, may hold values from 0.1 to 1.9
- proj_first: bfloat16 [6400, 4096], P('vis', ('row', 'col')), may hold values from -0.078125 to 0.078125
- proj_bias: float32 [4096], P(('row', 'col')), may hold values from -3 to 3
- proj_second: bfloat16 [4096, 4096], P(('row', 'col'), 'vis'), may hold values from -0.09375 to 0.09375
- gate_weight: bfloat16 [4096, 16384], P('vis', ('row', 'col')), may hold values from -0.09375 to 0.09375
- up_weight: bfloat16 [4096, 16384], P('vis', ('row', 'col')), may hold values from -0.09375 to 0.09375
- down_weight: bfloat16 [16384, 4096], P(('row', 'col'), 'vis'), may hold values from -0.046875 to 0.046875
- cotangent: bfloat16 [64, 4096], P(('row', 'col'), 'vis'), may hold values from -6 to 6
Outputs:
- block_out: bfloat16 [64, 4096], P(('row', 'col'), 'vis')
- image_slot_gradients: float32 [128, 6400], P(('vis', 'row', 'col'))
- first_grad: float32 [6400, 4096], P('vis', ('row', 'col'))
- second_grad: float32 [4096, 4096], P(('row', 'col'), 'vis')
Inputs may be any that keep to these rules, and one draw needn't show every extreme that they name: Vision device v's live rows are its first counts[v] slots; the counts sum to 64, and some device's slots are all live. `block_order`: each vision device's index once: the order in which the devices' live rows follow one another among the language rows.
All inputs are finite; a program needn't handle non-finite values.
Results may differ from a plain program's by a relative error of at most 0.034.
Values may be sent and summed in bfloat16 or wider, within the bound.
A program may use at most 64 MiB of HBM per device.

v0:
```python
import jax
import jax.numpy as jnp
from jax import lax
from jax.sharding import PartitionSpec as P


def row_tables(counts, block_order, total_rows, per_device, group_size):
    vision = counts.shape[0]
    labels = jnp.arange(vision, dtype=jnp.int32)
    chosen = (block_order[:, None] == labels[None, :]).astype(jnp.int32)
    ordered = jnp.sum(chosen * counts[None, :], axis=1)
    block_ends = jnp.cumsum(ordered)
    block_starts = block_ends - ordered
    language = jnp.arange(total_rows, dtype=jnp.int32)
    block_of = jnp.sum((block_ends[None, :] <= language[:, None]).astype(jnp.int32), axis=1)
    picked = (block_of[:, None] == labels[None, :]).astype(jnp.int32)
    owner = jnp.sum(picked * block_order[None, :], axis=1)
    offset = language - jnp.sum(picked * block_starts[None, :], axis=1)
    stride = vision * per_device
    source = offset // per_device * stride + owner * per_device + offset % per_device
    slots = jnp.arange(stride * group_size, dtype=jnp.int32)
    within = slots % stride
    slot_owner = within // per_device
    slot_offset = slots // stride * per_device + within % per_device
    owner_start = jnp.sum(chosen * block_starts[:, None], axis=0)
    matched = (slot_owner[:, None] == labels[None, :]).astype(jnp.int32)
    start_of = jnp.sum(matched * owner_start[None, :], axis=1)
    count_of = jnp.sum(matched * counts[None, :], axis=1)
    live = slot_offset < count_of
    target = jnp.where(live, start_of + slot_offset, 0)
    return (source, target, live)


def gelu_parts(pre):
    normal_cdf = 0.5 * (1.0 + jax.scipy.special.erf(pre * 0.7071067811865476))
    density = jnp.exp(-0.5 * pre * pre) * 0.3989422804014327
    return (pre * normal_cdf, normal_cdf + pre * density)


def apply_layer_norm(images, projector_norm_gain):
    values = images.astype(jnp.float32)
    mean_removed = values - jnp.mean(values, axis=-1, keepdims=True)
    variance = jnp.mean(mean_removed * mean_removed, axis=-1, keepdims=True)
    inverse_scale = lax.rsqrt(variance + 1e-05)
    standardized_input = mean_removed * inverse_scale
    return (
        standardized_input,
        inverse_scale,
        (standardized_input * projector_norm_gain).astype(jnp.bfloat16),
    )


def norm_gradient_pass(gradient_tuple, standardized_input, inverse_scale, projector_norm_gain):
    gain_scaled = gradient_tuple * projector_norm_gain
    return inverse_scale * (
        gain_scaled
        - jnp.mean(gain_scaled, axis=-1, keepdims=True)
        - standardized_input * jnp.mean(gain_scaled * standardized_input, axis=-1, keepdims=True)
    )


def product(left, right):
    return jnp.dot(left, right, preferred_element_type=jnp.float32)


def feed_grads(hidden_grad, gate_sum, up_sum, gate_sigmoid):
    gate_grad = (
        hidden_grad * up_sum * gate_sigmoid * (1.0 + gate_sum * (1.0 - gate_sigmoid))
    ).astype(jnp.bfloat16)
    up_grad = (hidden_grad * gate_sum * gate_sigmoid).astype(jnp.bfloat16)
    return (gate_grad, up_grad)


def on_device(
    images,
    counts,
    block_order,
    projector_norm_gain,
    proj_first,
    proj_bias,
    proj_second,
    gate_weight,
    up_weight,
    down_weight,
    cotangent,
):
    group_size = lax.axis_size(("row", "col"))
    per_device = images.shape[0]
    local_rows = cotangent.shape[0]
    total_rows = local_rows * group_size
    position = lax.axis_index(("row", "col"))
    source, target, live = row_tables(counts, block_order, total_rows, per_device, group_size)
    standardized_input, inverse_scale, norm_output = apply_layer_norm(images, projector_norm_gain)
    columns = lax.all_to_all(norm_output, "vis", split_axis=1, concat_axis=0, tiled=True)
    gathered = lax.all_gather(columns, ("row", "col"), axis=0, tiled=True)
    first_part = jnp.take(product(gathered, proj_first), source, axis=0)
    pre = lax.psum(first_part.astype(jnp.bfloat16), "vis").astype(jnp.float32) + proj_bias
    activated, slope = gelu_parts(pre)
    hidden_proj = activated.astype(jnp.bfloat16)
    inputs = lax.psum(product(hidden_proj, proj_second).astype(jnp.bfloat16), ("row", "col"))
    gate_part = product(inputs, gate_weight)
    up_part = product(inputs, up_weight)
    gate_sum, up_sum = (
        lax.psum(gate_part.astype(jnp.bfloat16), "vis").astype(jnp.float32),
        lax.psum(up_part.astype(jnp.bfloat16), "vis").astype(jnp.float32),
    )
    gate_sigmoid = jax.nn.sigmoid(gate_sum)
    hidden = (gate_sum * gate_sigmoid * up_sum).astype(jnp.bfloat16)
    block_part = lax.psum_scatter(
        product(hidden, down_weight).astype(jnp.bfloat16),
        ("row", "col"),
        scatter_dimension=0,
        tiled=True,
    ).astype(jnp.float32)
    own_inputs = lax.dynamic_slice_in_dim(inputs, position * local_rows, local_rows, 0)
    block_out = (own_inputs.astype(jnp.float32) + block_part).astype(jnp.bfloat16)
    upstream = lax.all_gather(cotangent, ("row", "col"), axis=0, tiled=True)
    hidden_part = product(upstream, down_weight.T)
    hidden_grad = lax.psum(hidden_part.astype(jnp.bfloat16), "vis").astype(jnp.float32)
    gate_grad, up_grad = feed_grads(hidden_grad, gate_sum, up_sum, gate_sigmoid)
    input_part = product(gate_grad, gate_weight.T) + product(up_grad, up_weight.T)
    input_grad = (
        upstream.astype(jnp.float32)
        + lax.psum(input_part.astype(jnp.bfloat16), ("row", "col")).astype(jnp.float32)
    ).astype(jnp.bfloat16)
    second_grad = product(hidden_proj.T, input_grad)
    pre_part = product(input_grad, proj_second.T)
    pre_grad = lax.psum(pre_part.astype(jnp.bfloat16), "vis").astype(jnp.float32)
    act_grad = (pre_grad * slope).astype(jnp.bfloat16)
    slot_act = jnp.where(
        live[:, None], jnp.take(act_grad, target, axis=0), jnp.zeros((), jnp.bfloat16)
    )
    first_grad = product(gathered.T, slot_act)
    slot_part = lax.psum_scatter(
        product(slot_act, proj_first.T).astype(jnp.bfloat16),
        ("row", "col"),
        scatter_dimension=0,
        tiled=True,
    ).astype(jnp.float32)
    return_values = lax.all_to_all(slot_part, "vis", split_axis=0, concat_axis=1, tiled=True)
    image_slot_gradients = norm_gradient_pass(
        return_values, standardized_input, inverse_scale, projector_norm_gain
    )
    return (block_out, image_slot_gradients, first_grad, second_grad)


def solution(mesh):
    in_specs = (
        P(("vis", "row", "col"), None),
        P(),
        P(),
        P(),
        P("vis", ("row", "col")),
        P(("row", "col")),
        P(("row", "col"), "vis"),
        P("vis", ("row", "col")),
        P("vis", ("row", "col")),
        P(("row", "col"), "vis"),
        P(("row", "col"), "vis"),
    )
    out_specs = (
        P(("row", "col"), "vis"),
        P(("vis", "row", "col"), None),
        P("vis", ("row", "col")),
        P(("row", "col"), "vis"),
    )
    return jax.shard_map(
        on_device, mesh=mesh, in_specs=in_specs, out_specs=out_specs, check_vma=False
    )
```

profile of v0, /device:TPU:0, one launch (start us, length us, event | category | flops | bytes accessed | tf_op | source)
XLA Modules:
  0.0 442.7 jit_solution(14485268734717426963)
XLA Ops:
  7.2 1.1 convert_reduce_fusion
  8.3 1.0 fusion.33
  9.4 0.9 fusion.29
  10.3 0.1 all_to_all.30
  10.4 0.6 copy.18
  11.1 4.3 all-to-all-start
  15.3 0.9 select_reduce_fusion.5
  16.2 0.2 reduce-window.7
  16.4 0.1 convert_reduce_fusion.1
  16.5 0.7 select_reduce_fusion.3
  17.3 2.1 all-to-all-done
  19.4 32.0 %all_gather.6 = bf16[128,1600]{1,0:T(8,128)(2,1)S(1)} all-gather(bf16[16,1600]{1,0:T(8,128)(2,1)S(1)} %all_to_all.33), channel_id=1, replica_groups=mesh['vis'=4,'row'=4,'col'=2] {'row','col'}, dimensions={0}, use_global_device_ids=true | all-gather | bytes 460800 | tf_op jit(solution)/shard_map/all_gather | solution.py:95
  51.4 0.4 fusion.49
  51.8 0.7 gather_fusion
  52.5 0.7 select_convert_fusion
  53.2 0.0 all-reduce.9.cloned.1.call-start
  53.3 30.7 %all_gather.7 = bf16[64,1024]{1,0:T(8,128)(2,1)S(1)} all-gather(bf16[8,1024]{1,0:T(8,128)(2,1)} %param.21), channel_id=1, replica_groups=mesh['vis'=4,'row'=4,'col'=2] {'row','col'}, dimensions={0}, use_global_device_ids=true | all-gather | bytes 147456 | tf_op jit(solution)/shard_map/all_gather | solution.py:117
  84.0 1.0 all-reduce.7.cloned.1.call-done
  85.0 1.8 convolution_convert_fusion.5
  86.9 4.3 convolution_convert_fusion.1
  91.2 0.1 select_reduce_fusion.1
  91.3 68.2 %all-reduce.9.cloned.1.call-done = bf16[64,1024]{1,0:T(8,128)(2,1)} async-done(((bf16[64,1024]{1,0:T(8,128)(2,1)}), bf16[64,1024]{1,0:T(8,128)(2,1)}) %all-reduce.9.cloned.1.call-update) | async-done | bytes 131088 | tf_op jit(solution)/shard_map/psum | solution.py:100
  159.4 3.9 convolution_convert_fusion.2
  163.4 1.5 convolution_convert_fusion.3
  165.0 0.1 select_reduce_fusion.2
  165.1 34.1 %all-reduce.15.cloned.1.call-done = (bf16[64,2048]{1,0:T(8,128)(2,1)}, bf16[64,2048]{1,0:T(8,128)(2,1)}, bf16[64,2048]{1,0:T(8,128)(2,1)}) async-done(((bf16[64,2048]{1,0:T(8,128)(2,1)}, bf16[64,2048]{1,0:T(8,128)(2,1)}, bf16[64,2048]{1,0:T(8,128)(2,1)}), (bf16[64,2048]{1,0:T(8,128)(2,1)}, bf16[64,2048]{1,0:T(8,128)(2,1)}, bf16[64,2048]{1,0:T(8,128)(2,1)})) %all-reduce.15.cloned.1.call-update) | async-done | bytes 786448 | tf_op jit(solution)/shard_map/psum | solution.py:105
  199.3 4.0 fusion.13
  203.3 2.1 fusion
  205.4 70.6 %all-reduce.11.cloned.1.call-done = bf16[64,1024]{1,0:T(8,128)(2,1)} async-done(((bf16[64,1024]{1,0:T(8,128)(2,1)}), bf16[64,1024]{1,0:T(8,128)(2,1)}) %all-reduce.11.cloned.1.call-update) | async-done | bytes 131088 | tf_op jit(solution)/shard_map/psum | solution.py:124
  276.0 2.0 convolution_convert_fusion.6
  278.0 0.0 reduce-scatter.5.cloned.1.call-start
  278.0 31.3 %all-reduce.13.cloned.1.call-done = bf16[64,512]{1,0:T(8,128)(2,1)} async-done(((bf16[64,512]{1,0:T(8,128)(2,1)}), bf16[64,512]{1,0:T(8,128)(2,1)}) %all-reduce.13.cloned.1.call-update) | async-done | bytes 65552 | tf_op jit(solution)/shard_map/psum | solution.py:128
  309.4 0.9 fusion.23
  310.3 0.8 gather_fusion.1
  311.2 1.5 convolution_convert_fusion
  312.7 0.1 mul.268
  312.8 3.9 convolution_convert_fusion.4
  316.7 1.8 fusion.34
  318.5 2.4 fusion.48
  320.9 48.0 %reduce-scatter.5.cloned.1.call-done = bf16[16,1600]{1,0:T(8,128)(2,1)} async-done(((bf16[128,1600]{1,0:T(8,128)(2,1)}), bf16[16,1600]{1,0:T(8,128)(2,1)}) %reduce-scatter.5.cloned.1.call-update) | async-done | bytes 51216 | tf_op jit(solution)/shard_map/reduce_scatter | solution.py:134
  368.9 1.5 reshape.329
  370.4 3.3 all-to-all-start.1
  373.7 59.5 %reduce-scatter.3.cloned.1.call-done = bf16[8,1024]{1,0:T(8,128)(2,1)} async-done(((bf16[64,1024]{1,0:T(8,128)(2,1)}), bf16[8,1024]{1,0:T(8,128)(2,1)}) %reduce-scatter.3.cloned.1.call-update) | async-done | bytes 16400 | tf_op jit(solution)/shard_map/reduce_scatter | solution.py:109
  433.2 1.3 add_convert_fusion.3
  434.5 0.1 all_to_all.38
  434.7 0.2 fusion.30
  434.9 0.2 multiply_reduce_fusion
  435.1 0.8 fusion.32
  (54 shorter events, 0.5 us)
Async XLA Ops:
  7.2 44.2 %copy-start = (bf16[1600,512]{1,0:T(8,128)(2,1)S(1)}, bf16[1600,512]{1,0:T(8,128)(2,1)}, u32[]{:S(2)}) copy-start(bf16[1600,512]{1,0:T(8,128)(2,1)} %param.15) | copy-start | bytes 4915204
  7.2 77.8 %copy-start.3 = (bf16[512,1024]{1,0:T(8,128)(2,1)S(1)}, bf16[512,1024]{1,0:T(8,128)(2,1)}, u32[]{:S(2)}) copy-start(bf16[512,1024]{1,0:T(8,128)(2,1)} %param.17) | copy-start | bytes 3145732
  7.2 77.8 %copy-start.9 = (f32[512]{0:T(512)S(1)}, f32[512]{0:T(512)}, u32[]{:S(2)}) copy-start(f32[512]{0:T(512)} %param.16) | copy-start | bytes 6148
  11.1 8.3 %all-to-all-start = ((bf16[4,4,1600]{2,0,1:T(4,128)(2,1)}), bf16[4,4,1600]{2,0,1:T(4,128)(2,1)S(1)}, u32[]{:S(2)}, u32[]{:S(2)}) async-start(bf16[4,4,1600]{2,0,1:T(4,128)(2,1)} %copy.18), calls=%async_computation | async-start | bytes 106496 | tf_op jit(solution)/shard_map/all_to_all | solution.py:94
  15.3 69.7 %all-reduce.7.cloned.1.call-start = ((), (), s32[]{:S(2)}) async-start(), calls=%async_computation.4 | async-start | bytes 131072 | tf_op jit(solution)/shard_map/psum | solution.py:97
  51.4 39.8 %copy-start.10 = (s32[4]{0:T(128)S(1)}, s32[4]{0:T(128)}, u32[]{:S(2)}) copy-start(s32[4]{0:T(128)} %param.13) | copy-start | bytes 52
  53.2 106.2 %all-reduce.9.cloned.1.call-start = ((), (), s32[]{:S(2)}) async-start(), calls=%async_computation.5 | async-start | bytes 262144 | tf_op jit(solution)/shard_map/psum | solution.py:100
  86.8 112.4 %all-reduce.15.cloned.1.call-start = ((), (), s32[]{:S(2)}) async-start(), calls=%async_computation.10 | async-start | bytes 1572864 | tf_op jit(solution)/shard_map/psum | solution.py:105
  91.3 73.8 %copy-start.11 = (s32[4]{0:T(128)S(1)}, s32[4]{0:T(128)}, u32[]{:S(2)}) copy-start(s32[4]{0:T(128)} %param.12) | copy-start | bytes 52
  159.4 4.0 copy-start.1
  159.4 4.0 copy-start.5
  165.0 111.0 %all-reduce.11.cloned.1.call-start = ((), (), s32[]{:S(2)}) async-start(), calls=%async_computation.7 | async-start | bytes 262144 | tf_op jit(solution)/shard_map/psum | solution.py:124
  199.2 4.0 copy-start.2
  199.3 4.0 copy-start.12
  199.3 4.0 copy-start.13
  203.2 106.1 %copy-start.6 = (bf16[64,512]{1,0:T(8,128)(2,1)S(1)}, bf16[64,512]{1,0:T(8,128)(2,1)}, u32[]{:S(2)}) copy-start(bf16[64,512]{1,0:T(8,128)(2,1)} %all-reduce.7.cloned.1.call-done) | copy-start | bytes 196612
  205.3 107.4 %copy-start.8 = (f32[6400]{0:T(1024)S(1)}, f32[6400]{0:T(1024)}, u32[]{:S(2)}) copy-start(f32[6400]{0:T(1024)} %param.14) | copy-start | bytes 76804
  205.3 104.0 %all-reduce.13.cloned.1.call-start = ((), (), s32[]{:S(2)}) async-start(), calls=%async_computation.8 | async-start | bytes 131072 | tf_op jit(solution)/shard_map/psum | solution.py:128
  278.0 90.9 %reduce-scatter.5.cloned.1.call-start = ((), (), s32[]{:S(2)}) async-start(), calls=%async_computation.9 | async-start | bytes 479232 | tf_op jit(solution)/shard_map/reduce_scatter | solution.py:134
  311.1 5.5 %copy-start.7 = (bf16[64,1024]{1,0:T(8,128)(2,1)S(1)}, bf16[64,1024]{1,0:T(8,128)(2,1)}, u32[]{:S(2)}) copy-start(bf16[64,1024]{1,0:T(8,128)(2,1)} %all-reduce.11.cloned.1.call-done) | copy-start | bytes 393220
  312.6 120.5 %reduce-scatter.3.cloned.1.call-start = ((), (), s32[]{:S(2)}) async-start(), calls=%async_computation.6 | async-start | bytes 147456 | tf_op jit(solution)/shard_map/reduce_scatter | solution.py:109
  316.7 118.0 %copy-start.4 = (bf16[4,6400]{1,0:T(4,128)(2,1)S(1)}, bf16[4,6400]{1,0:T(4,128)(2,1)}, u32[]{:S(2)}) copy-start(bf16[4,6400]{1,0:T(4,128)(2,1)} %param.11) | copy-start | bytes 153604
  370.4 64.1 %all-to-all-start.1 = ((f32[4,4,1600]{2,1,0:T(4,128)}), f32[4,4,1600]{2,1,0:T(4,128)S(1)}, u32[]{:S(2)}, u32[]{:S(2)}) async-start(f32[4,4,1600]{2,1,0:T(4,128)} %reshape.329), calls=%async_computation.3 | async-start | bytes 212992 | tf_op jit(solution)/shard_map/all_to_all | solution.py:140
Sparse Core Ops, SparseCore 0:
  53.3 31.6 all-reduce.6
  88.9 70.4 all-reduce.8
  165.1 34.1 all-reduce.14
  205.5 70.4 all-reduce.10
  278.7 30.6 all-reduce.12
  312.8 56.1 reduce-scatter.4
  372.2 60.9 reduce-scatter.2
where the time goes:
time: 443 us
  waiting for transfers between devices  315 us (71%)
  blocking collectives  62.7 us (14%)
  matrix products  29.5 us (7%)
  between operations  14.3 us (3%)
  other arithmetic  9.34 us (2%)
  starting transfers between devices  7.82 us (2%)
    psum x1, waiting for transfers between devices, on_device(): lax.psum(input_part.astype(jnp.bfloat16), ('row', 'col'))  70.6 us
    psum x1, waiting for transfers between devices, on_device(): lax.psum(product(hidden_proj, proj_second).astype(jnp.bfloat16), ('row',...  68.2 us
    reduce_scatter x1, waiting for transfers between devices, on_device(): lax.psum_scatter(product(hidden, down_weight).astype(jnp.bfloat16), ('row...  59.5 us
    reduce_scatter x1, waiting for transfers between devices, on_device(): lax.psum_scatter(product(slot_act, proj_first.T).astype(jnp.bfloat16), ('...  48 us
    psum x1, waiting for transfers between devices, on_device(): lax.psum(up_part.astype(jnp.bfloat16), 'vis').astype(jnp.float32)  34.1 us
    all_gather x1, blocking collectives, on_device(): gathered = lax.all_gather(columns, ('row', 'col'), axis=0, tiled=True)  32 us
    psum x1, waiting for transfers between devices, on_device(): lax.psum(pre_part.astype(jnp.bfloat16), 'vis').astype(jnp.float32)  31.3 us
    all_gather x1, blocking collectives, on_device(): upstream = lax.all_gather(cotangent, ('row', 'col'), axis=0, tiled=True)  30.7 us
  transfers between devices with their start and end apart: 9, of which 8 were waited for; matrix products, arithmetic and copies ran while one was open for 4% of the time, Pallas kernels for 0%

commit v1 on v0

--- a/solution.py
+++ b/solution.py
@@ -2,6 +2,11 @@
 import jax.numpy as jnp
 from jax import lax
 from jax.sharding import PartitionSpec as P
+
+
+def add_all(shard, axis):
+    parts = lax.all_gather(shard, axis)
+    return jnp.sum(parts, axis=0)
 
 
 def row_tables(counts, block_order, total_rows, per_device, group_size):
@@ -121,7 +126,7 @@
     input_part = product(gate_grad, gate_weight.T) + product(up_grad, up_weight.T)
     input_grad = (
         upstream.astype(jnp.float32)
-        + lax.psum(input_part.astype(jnp.bfloat16), ("row", "col")).astype(jnp.float32)
+        + add_all(input_part.astype(jnp.bfloat16), ("row", "col")).astype(jnp.float32)
     ).astype(jnp.bfloat16)
     second_grad = product(hidden_proj.T, input_grad)
     pre_part = product(input_grad, proj_second.T)

time: 443 us -> 421 us (0.950)
  waiting for transfers between devices: 315 us -> 292 us
    psum x1 -> x0, waiting for transfers between devices: 70.6 us -> none  [on_device(): lax.psum(input_part.astype(jnp.bfloat16), ('row', 'col'))]
    all_gather x0 -> x1, waiting for transfers between devices: none -> 40.1 us  [add_all(): parts = lax.all_gather(shard, axis)]
    reduce_scatter x1, waiting for transfers between devices: 48 us -> 55.8 us  [on_device(): lax.psum_scatter(product(slot_act, proj_first.T).astype(jnp.bfloat16), ('...]
    psum x1, waiting for transfers between devices: 31.3 us -> 26.5 us  [on_device(): lax.psum(pre_part.astype(jnp.bfloat16), 'vis').astype(jnp.float32)]
  transfers between devices with their start and end apart: 9 -> 9, of which waited for: 8 -> 9; matrix products, arithmetic and copies ran while one was open for 4% -> 5% of each run, Pallas kernels for 0% -> 0%
where the time goes in v1:
time: 421 us
  waiting for transfers between devices  292 us (69%)
  blocking collectives  62.7 us (15%)
  matrix products  28.6 us (7%)
  between operations  14.3 us (3%)
  other arithmetic  10.8 us (3%)
  starting transfers between devices  7.83 us (2%)
    psum x1, waiting for transfers between devices, on_device(): lax.psum(product(hidden_proj, proj_second).astype(jnp.bfloat16), ('row',...  68.3 us
    reduce_scatter x1, waiting for transfers between devices, on_device(): lax.psum_scatter(product(hidden, down_weight).astype(jnp.bfloat16), ('row...  62.2 us
    reduce_scatter x1, waiting for transfers between devices, on_device(): lax.psum_scatter(product(slot_act, proj_first.T).astype(jnp.bfloat16), ('...  55.8 us
    all_gather x1, waiting for transfers between devices, add_all(): parts = lax.all_gather(shard, axis)  40.1 us
    psum x1, waiting for transfers between devices, on_device(): lax.psum(up_part.astype(jnp.bfloat16), 'vis').astype(jnp.float32)  34.2 us
    all_gather x1, blocking collectives, on_device(): gathered = lax.all_gather(columns, ('row', 'col'), axis=0, tiled=True)  32 us
    all_gather x1, blocking collectives, on_device(): upstream = lax.all_gather(cotangent, ('row', 'col'), axis=0, tiled=True)  30.7 us
    dot_general x12, matrix products, product(): return jnp.dot(left, right, preferred_element_type=jnp.float32)  28.6 us
  transfers between devices with their start and end apart: 9, of which 9 were waited for; matrix products, arithmetic and copies ran while one was open for 5% of the time, Pallas kernels for 0%

profile of v1, /device:TPU:0, one launch (start us, length us, event | category | flops | bytes accessed | tf_op | source)
XLA Modules:
  0.0 420.7 jit_solution(10583916194462371126)
XLA Ops:
  7.2 1.1 convert_reduce_fusion
  8.3 1.0 fusion.33
  9.4 0.9 fusion.29
  10.3 0.1 all_to_all.30
  10.4 0.6 copy.18
  11.1 4.3 %all-to-all-start = ((bf16[4,4,1600]{2,0,1:T(4,128)(2,1)}), bf16[4,4,1600]{2,0,1:T(4,128)(2,1)S(1)}, u32[]{:S(2)}, u32[]{:S(2)}) async-start(bf16[4,4,1600]{2,0,1:T(4,128)(2,1)} %copy.18), calls=%async_computation | async-start | bytes 106496 | tf_op jit(solution)/shard_map/all_to_all | solution.py:99
  15.3 0.9 select_reduce_fusion.5
  16.2 0.2 reduce-window.7
  16.4 0.1 convert_reduce_fusion.1
  16.5 0.7 select_reduce_fusion.3
  17.3 2.1 all-to-all-done
  19.4 32.0 %all_gather.12 = bf16[128,1600]{1,0:T(8,128)(2,1)S(1)} all-gather(bf16[16,1600]{1,0:T(8,128)(2,1)S(1)} %all_to_all.33), channel_id=1, replica_groups=mesh['vis'=4,'row'=4,'col'=2] {'row','col'}, dimensions={0}, use_global_device_ids=true | all-gather | bytes 460800 | tf_op jit(solution)/shard_map/all_gather | solution.py:100
  51.4 0.4 fusion.49
  51.8 0.7 gather_fusion
  52.5 0.7 select_convert_fusion
  53.3 30.7 %all_gather.13 = bf16[64,1024]{1,0:T(8,128)(2,1)S(1)} all-gather(bf16[8,1024]{1,0:T(8,128)(2,1)} %param.21), channel_id=1, replica_groups=mesh['vis'=4,'row'=4,'col'=2] {'row','col'}, dimensions={0}, use_global_device_ids=true | all-gather | bytes 147456 | tf_op jit(solution)/shard_map/all_gather | solution.py:122
  84.0 1.0 all-reduce.6.cloned.1.call-done
  85.0 1.8 convolution_convert_fusion.5
  86.9 4.3 %convolution_convert_fusion.1 = bf16[64,2048]{1,0:T(8,128)(2,1)} fusion(bf16[64,1024]{1,0:T(8,128)(2,1)S(1)} %all_gather.13, bf16[2048,1024]{1,0:T(8,128)(2,1)} %param.20), kind=kOutput, calls=%fused_computation.3 | convolution fusion | flops 268566528 | bytes 4587520 | tf_op jit(solution)/shard_map/dot_general | solution.py:68
  91.2 68.3 %all-reduce.8.cloned.1.call-done = bf16[64,1024]{1,0:T(8,128)(2,1)} async-done(((bf16[64,1024]{1,0:T(8,128)(2,1)}), bf16[64,1024]{1,0:T(8,128)(2,1)}) %all-reduce.8.cloned.1.call-update) | async-done | bytes 131088 | tf_op jit(solution)/shard_map/psum | solution.py:105
  159.4 3.9 convolution_convert_fusion.2
  163.4 1.5 convolution_convert_fusion.3
  165.0 34.2 %all-reduce.12.cloned.1.call-done = (bf16[64,2048]{1,0:T(8,128)(2,1)}, bf16[64,2048]{1,0:T(8,128)(2,1)}, bf16[64,2048]{1,0:T(8,128)(2,1)}) async-done(((bf16[64,2048]{1,0:T(8,128)(2,1)}, bf16[64,2048]{1,0:T(8,128)(2,1)}, bf16[64,2048]{1,0:T(8,128)(2,1)}), (bf16[64,2048]{1,0:T(8,128)(2,1)}, bf16[64,2048]{1,0:T(8,128)(2,1)}, bf16[64,2048]{1,0:T(8,128)(2,1)})) %all-reduce.12.cloned.1.call-update) | async-done | bytes 786448 | tf_op jit(solution)/shard_map/psum | solution.py:110
  199.3 4.0 fusion.13
  203.3 2.1 fusion
  205.4 0.1 select_reduce_fusion.1
  205.5 0.1 select_reduce_fusion.2
  205.7 40.1 %all-gather.3.cloned.1.call-done = bf16[512,1024]{1,0:T(8,128)(2,1)} async-done(((bf16[64,1024]{1,0:T(8,128)(2,1)}), bf16[512,1024]{1,0:T(8,128)(2,1)}) %all-gather.3.cloned.1.call-update) | async-done | bytes 1048592 | tf_op jit(solution)/shard_map/all_gather | solution.py:8
  245.8 1.4 reduce_sum.127
  247.2 1.1 convolution_convert_fusion.6
  248.4 3.9 convolution_convert_fusion.4
  252.3 26.5 %all-reduce.10.cloned.1.call-done = bf16[64,512]{1,0:T(8,128)(2,1)} async-done(((bf16[64,512]{1,0:T(8,128)(2,1)}), bf16[64,512]{1,0:T(8,128)(2,1)}) %all-reduce.10.cloned.1.call-update) | async-done | bytes 65552 | tf_op jit(solution)/shard_map/psum | solution.py:133
  278.8 0.9 fusion.23
  279.7 0.8 gather_fusion.1
  280.6 1.5 convolution_convert_fusion
  282.1 0.1 mul.268
  282.2 62.2 %reduce-scatter.3.cloned.1.call-done = bf16[8,1024]{1,0:T(8,128)(2,1)} async-done(((bf16[64,1024]{1,0:T(8,128)(2,1)}), bf16[8,1024]{1,0:T(8,128)(2,1)}) %reduce-scatter.3.cloned.1.call-update) | async-done | bytes 16400 | tf_op jit(solution)/shard_map/reduce_scatter | solution.py:114
  344.4 1.3 add_convert_fusion.3
  345.7 1.8 fusion.34
  347.5 55.8 %reduce-scatter.5.cloned.1.call-done = bf16[16,1600]{1,0:T(8,128)(2,1)} async-done(((bf16[128,1600]{1,0:T(8,128)(2,1)}), bf16[16,1600]{1,0:T(8,128)(2,1)}) %reduce-scatter.5.cloned.1.call-update) | async-done | bytes 51216 | tf_op jit(solution)/shard_map/reduce_scatter | solution.py:139
  403.4 1.5 reshape.329
  404.8 3.3 all-to-all-start.1
  408.2 2.4 fusion.48
  410.5 1.9 all-to-all-done.1
  412.5 0.1 all_to_all.38
  412.7 0.2 fusion.30
  412.9 0.2 multiply_reduce_fusion
  413.1 0.8 fusion.32
  (53 shorter events, 0.6 us)
Async XLA Ops:
  7.2 44.2 %copy-start = (bf16[1600,512]{1,0:T(8,128)(2,1)S(1)}, bf16[1600,512]{1,0:T(8,128)(2,1)}, u32[]{:S(2)}) copy-start(bf16[1600,512]{1,0:T(8,128)(2,1)} %param.15) | copy-start | bytes 4915204
  7.2 77.8 %copy-start.3 = (bf16[512,1024]{1,0:T(8,128)(2,1)S(1)}, bf16[512,1024]{1,0:T(8,128)(2,1)}, u32[]{:S(2)}) copy-start(bf16[512,1024]{1,0:T(8,128)(2,1)} %param.17) | copy-start | bytes 3145732
  7.2 77.8 %copy-start.8 = (f32[512]{0:T(512)S(1)}, f32[512]{0:T(512)}, u32[]{:S(2)}) copy-start(f32[512]{0:T(512)} %param.16) | copy-start | bytes 6148
  11.1 8.3 %all-to-all-start = ((bf16[4,4,1600]{2,0,1:T(4,128)(2,1)}), bf16[4,4,1600]{2,0,1:T(4,128)(2,1)S(1)}, u32[]{:S(2)}, u32[]{:S(2)}) async-start(bf16[4,4,1600]{2,0,1:T(4,128)(2,1)} %copy.18), calls=%async_computation | async-start | bytes 106496 | tf_op jit(solution)/shard_map/all_to_all | solution.py:99
  15.3 69.7 %all-reduce.6.cloned.1.call-start = ((), (), s32[]{:S(2)}) async-start(), calls=%async_computation.4 | async-start | bytes 131072 | tf_op jit(solution)/shard_map/psum | solution.py:102
  53.2 106.2 %all-reduce.8.cloned.1.call-start = ((), (), s32[]{:S(2)}) async-start(), calls=%async_computation.5 | async-start | bytes 262144 | tf_op jit(solution)/shard_map/psum | solution.py:105
  86.8 112.4 %all-reduce.12.cloned.1.call-start = ((), (), s32[]{:S(2)}) async-start(), calls=%async_computation.10 | async-start | bytes 1572864 | tf_op jit(solution)/shard_map/psum | solution.py:110
  159.4 4.0 copy-start.1
  159.4 4.0 copy-start.5
  165.0 80.8 %all-gather.3.cloned.1.call-start = ((), (), s32[]{:S(2)}) async-start(), calls=%async_computation.9 | async-start | bytes 1179648 | tf_op jit(solution)/shard_map/all_gather | solution.py:8
  199.3 4.0 copy-start.2
  199.3 4.0 copy-start.11
  199.3 4.0 copy-start.12
  203.3 2.2 copy-start.9
  203.3 2.3 copy-start.10
  205.4 73.4 %all-reduce.10.cloned.1.call-start = ((), (), s32[]{:S(2)}) async-start(), calls=%async_computation.7 | async-start | bytes 131072 | tf_op jit(solution)/shard_map/psum | solution.py:133
  248.3 30.5 %copy-start.6 = (bf16[64,512]{1,0:T(8,128)(2,1)S(1)}, bf16[64,512]{1,0:T(8,128)(2,1)}, u32[]{:S(2)}) copy-start(bf16[64,512]{1,0:T(8,128)(2,1)} %all-reduce.6.cloned.1.call-done) | copy-start | bytes 196612
  248.3 33.8 %copy-start.7 = (f32[6400]{0:T(1024)S(1)}, f32[6400]{0:T(1024)}, u32[]{:S(2)}) copy-start(f32[6400]{0:T(1024)} %param.14) | copy-start | bytes 76804
  248.3 96.1 %reduce-scatter.3.cloned.1.call-start = ((), (), s32[]{:S(2)}) async-start(), calls=%async_computation.6 | async-start | bytes 147456 | tf_op jit(solution)/shard_map/reduce_scatter | solution.py:114
  252.3 151.1 %reduce-scatter.5.cloned.1.call-start = ((), (), s32[]{:S(2)}) async-start(), calls=%async_computation.8 | async-start | bytes 479232 | tf_op jit(solution)/shard_map/reduce_scatter | solution.py:139
  282.0 130.6 %copy-start.4 = (bf16[4,6400]{1,0:T(4,128)(2,1)S(1)}, bf16[4,6400]{1,0:T(4,128)(2,1)}, u32[]{:S(2)}) copy-start(bf16[4,6400]{1,0:T(4,128)(2,1)} %param.11) | copy-start | bytes 153604
  404.8 7.6 %all-to-all-start.1 = ((f32[4,4,1600]{2,1,0:T(4,128)}), f32[4,4,1600]{2,1,0:T(4,128)S(1)}, u32[]{:S(2)}, u32[]{:S(2)}) async-start(f32[4,4,1600]{2,1,0:T(4,128)} %reshape.329), calls=%async_computation.3 | async-start | bytes 212992 | tf_op jit(solution)/shard_map/all_to_all | solution.py:145
Sparse Core Ops, SparseCore 0:
  53.3 31.6 all-reduce.5
  88.9 70.4 all-reduce.7
  165.1 34.1 all-reduce.11
  205.5 40.2 all-gather.2
  248.5 30.2 all-reduce.9
  282.6 61.8 reduce-scatter.2
  348.2 55.1 reduce-scatter.4
